TPU v7x, 256 devices: a whole 4x4x8 slice. The times are simulated.
256 devices in a mesh: nodes: 64 (over x, z, core), mp: 4 (over y).
Axes of the slice: x: 4, y: 4, z: 8, core: 2. Of those that a mesh axis runs over, the one named last changes fastest.
Arguments:
- tokens: bfloat16 [2048, 64, 768], P('nodes'), may hold values from -32 to 32
- w_query: bfloat16 [768, 768], P('mp'), may hold values from -0.5 to 0.5
- w_key: bfloat16 [768, 768], P('mp'), may hold values from -0.5 to 0.5
- w_value: bfloat16 [768, 768], P('mp'), may hold values from -0.21875 to 0.21875
- grad_out: bfloat16 [2048, 12, 4096], P('nodes', 'mp'), may hold values from -6 to 6
- owned_cls: bfloat16 [768, 131072], P('mp', 'nodes'), may hold values from -24 to 24
- send_rows: int32 [64, 64, 32], P('nodes'), may hold values from 0 to 2047
- neigh_slot: int32 [2048, 2, 32], P('nodes'), may hold values from 0 to 2047
- neigh_count: int32 [2048, 2], P('nodes'), may hold values from 1 to 32
Outputs:
- context: bfloat16 [2048, 12, 4096], P('nodes', 'mp')
- grad_query: float32 [768, 768], P('mp')
- grad_key: float32 [768, 768], P('mp')
- grad_value: float32 [768, 768], P('mp')
- grad_cls: float32 [768, 131072], P('mp', 'nodes')
Inputs may be any that keep to these rules, and one draw needn't show every extreme that they name: send_rows[o, r, :] are rows of owner o's own block; rows may repeat. `neigh_slot`: entries with k >= neigh_count[c, t] are not used.
All inputs are finite; a program needn't handle non-finite values.
Results may differ from a plain program's by a relative error of at most 0.012.
The roundings to bfloat16 on the way count: a program that leaves them out, or rounds other values in their place, can miss the bound.
Values may be sent and summed in bfloat16 or wider, within the bound.
No kernel may reach another device: no remote copies, remote signals or barrier semaphores. Data moves between devices by JAX's collectives and lax.ppermute only.
A program may use at most 128 MiB of HBM per device.

v0:
```python
import math
import jax
import jax.numpy as jnp
from jax import lax
from jax.sharding import PartitionSpec as P

HD = 64


def widen_columns(features):
    return lax.all_gather(features, "mp", axis=0, tiled=True)


def local_attend(tokens, virtual, w_query, w_key, w_value, grad_out):
    centres, length, model_width = tokens.shape
    local_width = w_query.shape[0]
    head_count = local_width // HD
    type_count = virtual.shape[1]
    span = type_count + length
    key_input = jnp.concatenate([virtual, tokens], axis=1)
    flat_tokens = tokens.reshape(-1, model_width)
    flat_keys = key_input.reshape(-1, model_width)
    queries = (
        jnp.einsum("nd,od->no", flat_tokens, w_query, preferred_element_type=jnp.float32)
        .astype(jnp.bfloat16)
        .reshape(centres, length, head_count, HD)
    )
    keys = (
        jnp.einsum("nd,od->no", flat_keys, w_key, preferred_element_type=jnp.float32)
        .astype(jnp.bfloat16)
        .reshape(centres, span, head_count, HD)
    )
    values = (
        jnp.einsum("nd,od->no", flat_keys, w_value, preferred_element_type=jnp.float32)
        .astype(jnp.bfloat16)
        .reshape(centres, span, head_count, HD)
    )
    score_scale = 1.0 / math.sqrt(HD)
    scores = (
        jnp.einsum("clhe,cmhe->chlm", queries, keys, preferred_element_type=jnp.float32)
        * score_scale
    )
    attn_probs = jax.nn.softmax(scores, axis=-1)
    probs_low = attn_probs.astype(jnp.bfloat16)
    context = jnp.einsum(
        "chlm,cmhe->chle", probs_low, values, preferred_element_type=jnp.float32
    ).astype(jnp.bfloat16)
    grad_heads = grad_out.reshape(centres, head_count, length, HD)
    prob_grads = jnp.einsum(
        "chle,cmhe->chlm", grad_heads, values, preferred_element_type=jnp.float32
    )
    value_grads = jnp.einsum(
        "chlm,chle->cmhe", probs_low, grad_heads, preferred_element_type=jnp.float32
    ).astype(jnp.bfloat16)
    score_grads = (
        attn_probs
        * (prob_grads - jnp.sum(prob_grads * attn_probs, axis=-1, keepdims=True))
        * score_scale
    )
    score_low = score_grads.astype(jnp.bfloat16)
    query_grads = jnp.einsum(
        "chlm,cmhe->clhe", score_low, keys, preferred_element_type=jnp.float32
    ).astype(jnp.bfloat16)
    key_grads = jnp.einsum(
        "chlm,clhe->cmhe", score_low, queries, preferred_element_type=jnp.float32
    ).astype(jnp.bfloat16)
    part_query = jnp.einsum(
        "no,nd->od",
        query_grads.reshape(-1, local_width),
        flat_tokens,
        preferred_element_type=jnp.float32,
    )
    part_key = jnp.einsum(
        "no,nd->od",
        key_grads.reshape(-1, local_width),
        flat_keys,
        preferred_element_type=jnp.float32,
    )
    part_value = jnp.einsum(
        "no,nd->od",
        value_grads.reshape(-1, local_width),
        flat_keys,
        preferred_element_type=jnp.float32,
    )
    virtual_key = key_grads[:, :type_count].reshape(-1, local_width)
    virtual_value = value_grads[:, :type_count].reshape(-1, local_width)
    virtual_grads = jnp.einsum(
        "no,od->dn", virtual_key, w_key, preferred_element_type=jnp.float32
    ) + jnp.einsum("no,od->dn", virtual_value, w_value, preferred_element_type=jnp.float32)
    return (
        context.reshape(centres, head_count, length * HD),
        part_query,
        part_key,
        part_value,
        virtual_grads,
    )


def body(tokens, w_query, w_key, w_value, grad_out, owned_cls, send_rows, neigh_slot, neigh_count):
    centres = tokens.shape[0]
    model_width = tokens.shape[2]
    local_width = owned_cls.shape[0]
    own_rows = owned_cls.shape[1]
    type_count = neigh_slot.shape[1]
    slot_width = neigh_slot.shape[2]
    send_flat = send_rows[0].reshape(-1)
    outgoing = jnp.take(owned_cls, send_flat, axis=1)
    fetched = lax.all_to_all(outgoing, "nodes", split_axis=1, concat_axis=1, tiled=True)
    slots_total = fetched.shape[1]
    pairs = centres * type_count
    counts = neigh_count.reshape(-1).astype(jnp.float32)
    live_mask = lax.broadcasted_iota(jnp.int32, neigh_slot.shape, 2) < neigh_count[:, :, None]
    live_float = live_mask.astype(jnp.float32).reshape(-1)
    pair_index = lax.broadcasted_iota(jnp.int32, (pairs, slot_width), 0).reshape(-1)
    mixing = (
        jnp.zeros((pairs, slots_total), jnp.float32)
        .at[pair_index, neigh_slot.reshape(-1)]
        .add(live_float)
    )
    mixing_low = mixing.astype(jnp.bfloat16)
    full_table = widen_columns(fetched)
    summed = jnp.einsum("dr,nr->dn", full_table, mixing_low, preferred_element_type=jnp.float32)
    virtual_cols = (summed / counts[None, :]).astype(jnp.bfloat16)
    virtual = virtual_cols.T.reshape(centres, type_count, model_width)
    context, part_query, part_key, part_value, virtual_grads = local_attend(
        tokens, virtual, w_query, w_key, w_value, grad_out
    )
    summed_weights = lax.psum((part_query, part_key, part_value), "nodes")
    shared_grad = (
        lax.psum_scatter(
            virtual_grads.astype(jnp.bfloat16), "mp", scatter_dimension=0, tiled=True
        ).astype(jnp.float32)
        / counts[None, :]
    )
    slot_grads = jnp.dot(
        shared_grad, mixing, precision=lax.Precision.HIGHEST, preferred_element_type=jnp.float32
    )
    returned = lax.all_to_all(
        slot_grads.astype(jnp.bfloat16), "nodes", split_axis=1, concat_axis=1, tiled=True
    ).astype(slot_grads.dtype)
    grad_cls = jnp.zeros((local_width, own_rows), jnp.float32).at[:, send_flat].add(returned)
    return (context, summed_weights[0], summed_weights[1], summed_weights[2], grad_cls)


def solution(mesh):
    in_specs = (
        P("nodes", None, None),
        P("mp", None),
        P("mp", None),
        P("mp", None),
        P("nodes", "mp", None),
        P("mp", "nodes"),
        P("nodes", None, None),
        P("nodes", None, None),
        P("nodes", None),
    )
    out_specs = (
        P("nodes", "mp", None),
        P("mp", None),
        P("mp", None),
        P("mp", None),
        P("mp", "nodes"),
    )
    return jax.shard_map(body, mesh=mesh, in_specs=in_specs, out_specs=out_specs, check_vma=False)
```

profile of v0, /device:TPU:8, one launch (start us, length us, event | category | flops | bytes accessed | tf_op | source)
XLA Modules:
  0.0 523.2 jit_solution(8477868783395647791)
XLA Ops:
  10.4 7.5 %gather_fusion = bf16[2048,192]{1,0:T(8,128)(2,1)S(1)} fusion(bf16[192,2048]{0,1:T(8,128)(2,1)S(1)} %copy.75, s32[2048]{0:T(1024)S(1)} %broadcast_clamp_fusion), kind=kCustom, calls=%fused_computation | custom fusion | bytes 1581056 | tf_op jit(solution)/shard_map/jit(_take)/gather | solution.py:107
  18.5 40.3 %all_to_all.18 = bf16[192,64,32]{0,2,1:T(8,128)(2,1)} all-to-all(bf16[192,64,32]{0,2,1:T(8,128)(2,1)S(1)} %broadcast_select_fusion), channel_id=1, replica_groups=mesh['nodes'=64,'mp'=4] {'nodes'}, dimensions={1} | all-to-all | bytes 1572864 | tf_op jit(solution)/shard_map/all_to_all | solution.py:108
  58.7 2.2 copy.76
  61.7 12.3 %scatter_custom_fusion.1 = f32[131072]{0:T(1024)} fusion(s32[2048]{0:T(1024)S(1)} %broadcast_select_fusion.1, f32[2048]{0:T(1024)S(1)} %reshape.213, f32[]{:T(128)} %constant.8.clone.1), kind=kCustom, calls=%fused_computation.49 | custom fusion | flops 2048 | bytes 524292
  74.0 1.9 reshape.192
  76.1 3.0 convolution_convert_fusion.2
  79.1 3.4 reshape.175
  82.6 3.5 reshape.183
  86.0 13.8 %all-gather.2.cloned.1.call-done = bf16[768,2048]{1,0:T(8,128)(2,1)} async-done(((bf16[192,2048]{1,0:T(8,128)(2,1)}), bf16[768,2048]{1,0:T(8,128)(2,1)}) %all-gather.2.cloned.1.call-update) | async-done | bytes 3145744 | tf_op jit(solution)/shard_map/all_gather | solution.py:11
  99.9 3.1 fusion.24
  103.7 4.6 pad_maximum_fusion
  108.3 3.1 reshape.179
  111.4 3.1 convolution_convert_fusion
  114.5 6.8 %reshape.181 = bf16[32,66,3,64]{1,0,3,2:T(8,128)(2,1)} reshape(bf16[2112,192]{0,1:T(8,128)(2,1)} %convolution_convert_fusion) | data formatting | bytes 1622016 | tf_op jit(solution)/shard_map/reshape | solution.py:36
  121.3 2.1 convolution_convert_fusion.1
  123.5 7.0 %reshape.180 = bf16[32,66,3,64]{1,0,3,2:T(8,128)(2,1)} reshape(bf16[2112,192]{0,1:T(8,128)(2,1)} %convolution_convert_fusion.1) | data formatting | bytes 1622016 | tf_op jit(solution)/shard_map/reshape | solution.py:31
  130.4 3.4 fusion.14
  133.9 3.2 fusion.49
  138.1 2.7 fusion.18
  140.7 39.7 %fusion.10 = bf16[32,64,3,64]{1,3,2,0:T(8,128)(2,1)} fusion(f32[32,3,66,64]{2,3,1,0:T(8,128)} %fusion.18, bf16[32,66,3,64]{1,0,3,2:T(8,128)(2,1)} %reshape.180, f32[32,3,64,66]{3,2,1,0:T(8,128)} %get-tuple-element.29, f32[32,3,64]{2,1,0:T(4,128)} %get-tuple-element.28), kind=kOutput, calls=%fused_computation.26 | convolution fusion | flops 55142464 | bytes 4866048 | tf_op jit(solution)/shard_map/chlm,cmhe->clhe/dot_general | solution.py:61
  180.5 40.3 %fusion.11 = bf16[32,66,3,64]{1,3,2,0:T(8,128)(2,1)} fusion(f32[32,3,66,64]{2,3,1,0:T(8,128)} %fusion.18, bf16[32,64,3,64]{1,0,3,2:T(8,128)(2,1)} %reshape.175, f32[32,3,64,66]{3,2,1,0:T(8,128)} %get-tuple-element.29, f32[32,3,64]{2,1,0:T(4,128)} %get-tuple-element.28), kind=kOutput, calls=%fused_computation.27 | convolution fusion | flops 55154752 | bytes 4866048 | tf_op jit(solution)/shard_map/chlm,clhe->cmhe/dot_general | solution.py:64
  220.7 15.9 %fusion.12 = bf16[32,66,3,64]{1,3,2,0:T(8,128)(2,1)} fusion(bf16[32,3,64,64]{3,2,0,1:T(8,128)(2,1)} %reshape.183, f32[32,3,64]{2,1,0:T(4,128)} %get-tuple-element.28, f32[32,3,64,66]{3,2,1,0:T(8,128)} %copy-done.2), kind=kOutput, calls=%fused_computation.28 | convolution fusion | flops 54343744 | bytes 3244032 | tf_op jit(solution)/shard_map/chlm,chle->cmhe/dot_general | solution.py:52
  236.6 3.6 copy.85
  240.2 3.5 reshape.184
  243.7 3.6 copy.87
  247.3 4.2 reshape.185
  251.4 3.6 copy.89
  255.0 4.2 reshape.186
  259.1 2.7 copy.90
  263.4 1.6 fusion.53
  265.0 2.8 copy.91
  269.4 1.9 fusion.26
  271.2 1.7 copy.97
  272.9 2.8 fusion.51
  275.8 19.8 %reduce-scatter.4.cloned.1.call-done = bf16[192,64]{1,0:T(8,128)(2,1)} async-done(((bf16[768,64]{1,0:T(8,128)(2,1)}), bf16[192,64]{1,0:T(8,128)(2,1)}) %reduce-scatter.4.cloned.1.call-update) | async-done | bytes 24592
  297.0 3.4 convolution_convert_fusion.3
  300.5 2.2 copy.92
  302.7 10.7 %all-to-all-start.1 = ((bf16[192,64,32]{0,2,1:T(8,128)(2,1)}), bf16[192,64,32]{0,2,1:T(8,128)(2,1)}, u32[]{:S(2)}, u32[]{:S(2)}) async-start(bf16[192,64,32]{0,2,1:T(8,128)(2,1)} %bitcast.91), calls=%async_computation.1 | async-start | bytes 2097152 | tf_op jit(solution)/shard_map/all_to_all | solution.py:138
  313.5 3.8 fusion.50
  317.3 1.7 fusion.52
  319.0 14.1 %convolution_convert_fusion.7 = bf16[32,3,64,64]{3,2,1,0:T(8,128)(2,1)S(1)} fusion(bf16[32,66,3,64]{1,0,3,2:T(8,128)(2,1)} %reshape.181, f32[32,3,64]{2,1,0:T(4,128)} %get-tuple-element.28, f32[32,3,64,66]{3,2,1,0:T(8,128)} %copy-done.2), kind=kOutput, calls=%fused_computation.23 | convolution fusion | flops 54331456 | bytes 3244032 | tf_op jit(solution)/shard_map/chlm,cmhe->chle/dot_general | solution.py:45
  336.0 5.9 %all-to-all-done.1 = bf16[192,64,32]{0,2,1:T(8,128)(2,1)} async-done(((bf16[192,64,32]{0,2,1:T(8,128)(2,1)}), bf16[192,64,32]{0,2,1:T(8,128)(2,1)}, u32[]{:S(2)}, u32[]{:S(2)}) %all-to-all-start.1) | async-done | bytes 786464 | tf_op jit(solution)/shard_map/all_to_all | solution.py:138
  341.8 11.4 %scatter_custom_fusion = f32[192,2048]{0,1:T(8,128)S(1)} fusion(s32[2048]{0:T(1024)S(1)} %bitcast.95, bf16[192,2048]{0,1:T(8,128)(2,1)} %bitcast.16, f32[]{:T(128)} %constant.8.clone.1), kind=kCustom, calls=%fused_computation.19 | custom fusion | flops 786432 | bytes 2359300 | tf_op jit(solution)/shard_map/scatter-add | solution.py:141
  353.3 1.7 copy.93
  355.0 155.8 %all-reduce.3.cloned.1.call-done = (f32[192,768]{1,0:T(8,128)}, f32[192,768]{1,0:T(8,128)}, f32[192,768]{1,0:T(8,128)}) async-done(((f32[192,768]{1,0:T(8,128)}, f32[192,768]{1,0:T(8,128)}, f32[192,768]{1,0:T(8,128)}), (f32[192,768]{1,0:T(8,128)}, f32[192,768]{1,0:T(8,128)}, f32[192,768]{1,0:T(8,128)})) %all-reduce.3.cloned.1.call-update) | async-done | bytes 1769488 | tf_op jit(solution)/shard_map/psum | solution.py:128
  510.7 1.9 copy.118
  512.7 1.9 copy.119
  514.6 1.9 copy.120
  (53 shorter events, 13.8 us)
Async XLA Ops:
  7.2 114.2 %copy-start = (bf16[192,768]{1,0:T(8,128)(2,1)S(1)}, bf16[192,768]{1,0:T(8,128)(2,1)}, u32[]{:S(2)}) copy-start(bf16[192,768]{1,0:T(8,128)(2,1)} %param.11) | copy-start | bytes 884740
  7.2 92.7 %all-gather.2.cloned.1.call-start = ((), (), s32[]{:S(2)}) async-start(), calls=%async_computation.3 | async-start | bytes 3932160 | tf_op jit(solution)/shard_map/all_gather | solution.py:11
  17.9 43.0 %copy-start.7 = (s32[32,2]{0,1:T(2,128)S(1)}, s32[32,2]{0,1:T(2,128)}, u32[]{:S(2)}) copy-start(s32[32,2]{0,1:T(2,128)} %param.17) | copy-start | bytes 772
  18.0 43.1 %copy-start.6 = (s32[32,2,32]{2,1,0:T(2,128)S(1)}, s32[32,2,32]{2,1,0:T(2,128)}, u32[]{:S(2)}) copy-start(s32[32,2,32]{2,1,0:T(2,128)} %param.16) | copy-start | bytes 24580
  18.0 43.5 %copy-start.8 = (s32[2]{0:T(128)S(1)}, s32[2]{0:T(128)}, u32[]{:S(2)}) copy-start(s32[2]{0:T(128)} %constant.34) | copy-start | bytes 28
  18.0 43.6 %copy-start.9 = (s32[2]{0:T(128)S(1)}, s32[2]{0:T(128)}, u32[]{:S(2)}) copy-start(s32[2]{0:T(128)} %constant.37) | copy-start | bytes 28
  18.5 57.7 %copy-start.1 = (bf16[32,64,768]{2,1,0:T(8,128)(2,1)S(1)}, bf16[32,64,768]{2,1,0:T(8,128)(2,1)}, u32[]{:S(2)}) copy-start(bf16[32,64,768]{2,1,0:T(8,128)(2,1)} %param.9) | copy-start | bytes 9437188
  60.9 234.6 %reduce-scatter.4.cloned.1.call-start = ((), (), s32[]{:S(2)}) async-start(), calls=%async_computation.4 | async-start | bytes 245760
  133.9 3.3 copy-start.2
  133.9 3.3 copy-start.3
  133.9 4.2 copy-start.4
  302.7 39.1 %all-to-all-start.1 = ((bf16[192,64,32]{0,2,1:T(8,128)(2,1)}), bf16[192,64,32]{0,2,1:T(8,128)(2,1)}, u32[]{:S(2)}, u32[]{:S(2)}) async-start(bf16[192,64,32]{0,2,1:T(8,128)(2,1)} %bitcast.91), calls=%async_computation.1 | async-start | bytes 2097152 | tf_op jit(solution)/shard_map/all_to_all | solution.py:138
  313.4 197.3 %all-reduce.3.cloned.1.call-start = ((), (), s32[]{:S(2)}) async-start(), calls=%async_computation.5 | async-start | bytes 3538944 | tf_op jit(solution)/shard_map/psum | solution.py:128
  313.5 3.8 copy-start.5
Sparse Core Ops, SparseCore 0:
  61.0 38.7 all-gather.1
  273.1 22.4 reduce-scatter.3
  319.1 191.5 all-reduce.2
where the time goes:
time: 528 us; the launch traced here: 523 us
  waiting for transfers between devices  195 us (37%)
  matrix products  143 us (27%)
  local copies, waits for them, and re-layouts  86.9 us (16%)
  blocking collectives  40.3 us (8%)
  other arithmetic  33.1 us (6%)
  between operations  14.3 us (3%)
  starting transfers between devices  10.8 us (2%)
    psum x1, waiting for transfers between devices, body(): summed_weights = lax.psum((part_query, part_key, part_value), 'nodes')  156 us
    dot_general x1, matrix products, local_attend(): jnp.einsum('chlm,clhe->cmhe', score_low, queries, preferred_element_type=...  40.3 us
    all_to_all x1, blocking collectives, body(): lax.all_to_all(outgoing, 'nodes', split_axis=1, concat_axis=1, tiled=True)  40.3 us
    dot_general x1, matrix products, local_attend(): jnp.einsum('chlm,cmhe->clhe', score_low, keys, preferred_element_type=jnp...  39.7 us
    unnamed x4, waiting for transfers between devices  19.8 us
    dot_general x1, matrix products, local_attend(): jnp.einsum('chlm,chle->cmhe', probs_low, grad_heads, preferred_element_ty...  15.9 us
    dot_general x1, matrix products, local_attend(): jnp.einsum('chlm,cmhe->chle', probs_low, values, preferred_element_type=j...  14.1 us
    unnamed x29, local copies, waits for them, and re-layouts  14 us
  transfers between devices with their start and end apart: 4, of which 4 were waited for; matrix products, arithmetic and copies ran while one was open for 12% of the time, Pallas kernels for 0%

commit v1 on v0

--- a/solution.py
+++ b/solution.py
@@ -105,7 +105,12 @@
     slot_width = neigh_slot.shape[2]
     send_flat = send_rows[0].reshape(-1)
     outgoing = jnp.take(owned_cls, send_flat, axis=1)
-    fetched = lax.all_to_all(outgoing, "nodes", split_axis=1, concat_axis=1, tiled=True)
+    fetched = jnp.concatenate(
+        lax.all_to_all(
+            jnp.stack(jnp.split(outgoing, lax.axis_size("nodes"), axis=1)), "nodes", 0, 0
+        ),
+        axis=1,
+    )
     slots_total = fetched.shape[1]
     pairs = centres * type_count
     counts = neigh_count.reshape(-1).astype(jnp.float32)

time: 528 us -> 528 us (level)
    unnamed x29 -> x92, local copies, waits for them, and re-layouts: 14 us -> 14.2 us
where the time goes in v1:
time: 528 us; the launch traced here: 523 us
  waiting for transfers between devices  195 us (37%)
  matrix products  143 us (27%)
  local copies, waits for them, and re-layouts  87.1 us (16%)
  blocking collectives  40.3 us (8%)
  other arithmetic  32.4 us (6%)
  between operations  14.8 us (3%)
  starting transfers between devices  10.8 us (2%)
    psum x1, waiting for transfers between devices, body(): summed_weights = lax.psum((part_query, part_key, part_value), 'nodes')  156 us
    dot_general x1, matrix products, local_attend(): jnp.einsum('chlm,clhe->cmhe', score_low, queries, preferred_element_type=...  40.3 us
    all_to_all x1, blocking collectives, body(): lax.all_to_all(jnp.stack(jnp.split(outgoing, lax.axis_size('nodes'), axis...  40.3 us
    dot_general x1, matrix products, local_attend(): jnp.einsum('chlm,cmhe->clhe', score_low, keys, preferred_element_type=jnp...  39.7 us
    unnamed x4, waiting for transfers between devices  19.8 us
    dot_general x1, matrix products, local_attend(): jnp.einsum('chlm,chle->cmhe', probs_low, grad_heads, preferred_element_ty...  15.9 us
    unnamed x92, local copies, waits for them, and re-layouts  14.2 us
    dot_general x1, matrix products, local_attend(): jnp.einsum('chlm,cmhe->chle', probs_low, values, preferred_element_type=j...  14.1 us
  transfers between devices with their start and end apart: 4, of which 4 were waited for; matrix products, arithmetic and copies ran while one was open for 12% of the time, Pallas kernels for 0%

profile of v1, /device:TPU:8, one launch (start us, length us, event | category | flops | bytes accessed | tf_op | source)
XLA Modules:
  0.0 523.2 jit_solution(7966686166117408120)
XLA Ops:
  9.7 7.5 %gather_fusion = bf16[2048,192]{1,0:T(8,128)(2,1)S(1)} fusion(bf16[192,2048]{0,1:T(8,128)(2,1)S(1)} %copy.52, s32[2048]{0:T(1024)S(1)} %broadcast_clamp_fusion), kind=kCustom, calls=%fused_computation | custom fusion | bytes 1581056 | tf_op jit(solution)/shard_map/jit(_take)/gather | solution.py:107
  18.5 40.3 %all_to_all.14 = bf16[64,192,32]{1,2,0:T(8,128)(2,1)} all-to-all(bf16[64,192,32]{1,2,0:T(8,128)(2,1)S(1)} %constant_dynamic-update-slice_fusion), channel_id=1, replica_groups=mesh['nodes'=64,'mp'=4] {'nodes'}, dimensions={0} | all-to-all | bytes 1572864 | tf_op jit(solution)/shard_map/all_to_all | solution.py:109
  58.7 2.2 copy.53
  61.7 12.3 %scatter_custom_fusion.1 = f32[131072]{0:T(1024)} fusion(s32[2048]{0:T(1024)S(1)} %broadcast_select_fusion, f32[2048]{0:T(1024)S(1)} %reshape.213, f32[]{:T(128)} %constant.8.clone.1), kind=kCustom, calls=%fused_computation.49 | custom fusion | flops 2048 | bytes 524292
  74.0 1.9 reshape.192
  76.1 3.0 convolution_convert_fusion.2
  79.1 3.4 reshape.173
  82.6 3.5 reshape.183
  86.0 13.8 %all-gather.2.cloned.1.call-done = bf16[768,2048]{1,0:T(8,128)(2,1)} async-done(((bf16[192,2048]{1,0:T(8,128)(2,1)}), bf16[768,2048]{1,0:T(8,128)(2,1)}) %all-gather.2.cloned.1.call-update) | async-done | bytes 3145744 | tf_op jit(solution)/shard_map/all_gather | solution.py:11
  99.9 3.1 fusion.24
  103.7 4.6 pad_maximum_fusion
  108.3 3.1 reshape.179
  111.4 3.1 convolution_convert_fusion
  114.5 6.8 %reshape.181 = bf16[32,66,3,64]{1,0,3,2:T(8,128)(2,1)} reshape(bf16[2112,192]{0,1:T(8,128)(2,1)} %convolution_convert_fusion) | data formatting | bytes 1622016 | tf_op jit(solution)/shard_map/reshape | solution.py:36
  121.3 2.1 convolution_convert_fusion.1
  123.5 7.0 %reshape.180 = bf16[32,66,3,64]{1,0,3,2:T(8,128)(2,1)} reshape(bf16[2112,192]{0,1:T(8,128)(2,1)} %convolution_convert_fusion.1) | data formatting | bytes 1622016 | tf_op jit(solution)/shard_map/reshape | solution.py:31
  130.4 3.4 fusion.14
  133.9 3.2 fusion.49
  138.1 2.7 fusion.18
  140.7 39.7 %fusion.10 = bf16[32,64,3,64]{1,3,2,0:T(8,128)(2,1)} fusion(f32[32,3,66,64]{2,3,1,0:T(8,128)} %fusion.18, bf16[32,66,3,64]{1,0,3,2:T(8,128)(2,1)} %reshape.180, f32[32,3,64,66]{3,2,1,0:T(8,128)} %get-tuple-element.24, f32[32,3,64]{2,1,0:T(4,128)} %get-tuple-element.23), kind=kOutput, calls=%fused_computation.26 | convolution fusion | flops 55142464 | bytes 4866048 | tf_op jit(solution)/shard_map/chlm,cmhe->clhe/dot_general | solution.py:61
  180.5 40.3 %fusion.11 = bf16[32,66,3,64]{1,3,2,0:T(8,128)(2,1)} fusion(f32[32,3,66,64]{2,3,1,0:T(8,128)} %fusion.18, bf16[32,64,3,64]{1,0,3,2:T(8,128)(2,1)} %reshape.173, f32[32,3,64,66]{3,2,1,0:T(8,128)} %get-tuple-element.24, f32[32,3,64]{2,1,0:T(4,128)} %get-tuple-element.23), kind=kOutput, calls=%fused_computation.27 | convolution fusion | flops 55154752 | bytes 4866048 | tf_op jit(solution)/shard_map/chlm,clhe->cmhe/dot_general | solution.py:64
  220.7 15.9 %fusion.12 = bf16[32,66,3,64]{1,3,2,0:T(8,128)(2,1)} fusion(bf16[32,3,64,64]{3,2,0,1:T(8,128)(2,1)} %reshape.183, f32[32,3,64]{2,1,0:T(4,128)} %get-tuple-element.23, f32[32,3,64,66]{3,2,1,0:T(8,128)} %copy-done.2), kind=kOutput, calls=%fused_computation.28 | convolution fusion | flops 54343744 | bytes 3244032 | tf_op jit(solution)/shard_map/chlm,chle->cmhe/dot_general | solution.py:52
  236.6 3.6 copy.62
  240.2 3.5 reshape.184
  243.7 3.6 copy.64
  247.3 4.2 reshape.185
  251.4 3.6 copy.66
  255.0 4.2 reshape.186
  259.2 2.7 copy.67
  263.4 1.6 fusion.53
  265.0 2.8 copy.68
  269.4 1.9 fusion.26
  271.2 1.7 copy.74
  272.9 2.8 fusion.51
  275.8 19.8 %reduce-scatter.4.cloned.1.call-done = bf16[192,64]{1,0:T(8,128)(2,1)} async-done(((bf16[768,64]{1,0:T(8,128)(2,1)}), bf16[192,64]{1,0:T(8,128)(2,1)}) %reduce-scatter.4.cloned.1.call-update) | async-done | bytes 24592
  297.1 3.4 convolution_convert_fusion.3
  300.5 2.2 copy.69
  302.7 10.7 %all-to-all-start.1 = ((bf16[192,64,32]{0,2,1:T(8,128)(2,1)}), bf16[192,64,32]{0,2,1:T(8,128)(2,1)}, u32[]{:S(2)}, u32[]{:S(2)}) async-start(bf16[192,64,32]{0,2,1:T(8,128)(2,1)} %bitcast.344), calls=%async_computation.1 | async-start | bytes 2097152 | tf_op jit(solution)/shard_map/all_to_all | solution.py:143
  313.5 3.8 fusion.50
  317.3 1.7 fusion.52
  319.0 14.1 %convolution_convert_fusion.7 = bf16[32,3,64,64]{3,2,1,0:T(8,128)(2,1)S(1)} fusion(bf16[32,66,3,64]{1,0,3,2:T(8,128)(2,1)} %reshape.181, f32[32,3,64]{2,1,0:T(4,128)} %get-tuple-element.23, f32[32,3,64,66]{3,2,1,0:T(8,128)} %copy-done.2), kind=kOutput, calls=%fused_computation.23 | convolution fusion | flops 54331456 | bytes 3244032 | tf_op jit(solution)/shard_map/chlm,cmhe->chle/dot_general | solution.py:45
  336.0 5.9 %all-to-all-done.1 = bf16[192,64,32]{0,2,1:T(8,128)(2,1)} async-done(((bf16[192,64,32]{0,2,1:T(8,128)(2,1)}), bf16[192,64,32]{0,2,1:T(8,128)(2,1)}, u32[]{:S(2)}, u32[]{:S(2)}) %all-to-all-start.1) | async-done | bytes 786464 | tf_op jit(solution)/shard_map/all_to_all | solution.py:143
  341.8 11.4 %scatter_custom_fusion = f32[192,2048]{0,1:T(8,128)S(1)} fusion(s32[2048]{0:T(1024)S(1)} %bitcast.347, bf16[192,2048]{0,1:T(8,128)(2,1)} %bitcast.79, f32[]{:T(128)} %constant.8.clone.1), kind=kCustom, calls=%fused_computation.19 | custom fusion | flops 786432 | bytes 2359300 | tf_op jit(solution)/shard_map/scatter-add | solution.py:146
  353.3 1.7 copy.70
  355.0 155.7 %all-reduce.3.cloned.1.call-done = (f32[192,768]{1,0:T(8,128)}, f32[192,768]{1,0:T(8,128)}, f32[192,768]{1,0:T(8,128)}) async-done(((f32[192,768]{1,0:T(8,128)}, f32[192,768]{1,0:T(8,128)}, f32[192,768]{1,0:T(8,128)}), (f32[192,768]{1,0:T(8,128)}, f32[192,768]{1,0:T(8,128)}, f32[192,768]{1,0:T(8,128)})) %all-reduce.3.cloned.1.call-update) | async-done | bytes 1769488 | tf_op jit(solution)/shard_map/psum | solution.py:133
  510.7 1.9 copy.158
  512.6 1.9 copy.159
  514.5 1.9 copy.160
  (117 shorter events, 13.3 us)
Async XLA Ops:
  7.2 114.2 %copy-start = (bf16[192,768]{1,0:T(8,128)(2,1)S(1)}, bf16[192,768]{1,0:T(8,128)(2,1)}, u32[]{:S(2)}) copy-start(bf16[192,768]{1,0:T(8,128)(2,1)} %param.11) | copy-start | bytes 884740
  7.2 92.7 %all-gather.2.cloned.1.call-start = ((), (), s32[]{:S(2)}) async-start(), calls=%async_computation.3 | async-start | bytes 3932160 | tf_op jit(solution)/shard_map/all_gather | solution.py:11
  17.9 43.1 %copy-start.7 = (s32[32,2]{0,1:T(2,128)S(1)}, s32[32,2]{0,1:T(2,128)}, u32[]{:S(2)}) copy-start(s32[32,2]{0,1:T(2,128)} %param.17) | copy-start | bytes 772
  17.9 43.2 %copy-start.6 = (s32[32,2,32]{2,1,0:T(2,128)S(1)}, s32[32,2,32]{2,1,0:T(2,128)}, u32[]{:S(2)}) copy-start(s32[32,2,32]{2,1,0:T(2,128)} %param.16) | copy-start | bytes 24580
  18.0 43.5 %copy-start.8 = (s32[2]{0:T(128)S(1)}, s32[2]{0:T(128)}, u32[]{:S(2)}) copy-start(s32[2]{0:T(128)} %constant.34) | copy-start | bytes 28
  18.0 43.6 %copy-start.9 = (s32[2]{0:T(128)S(1)}, s32[2]{0:T(128)}, u32[]{:S(2)}) copy-start(s32[2]{0:T(128)} %constant.37) | copy-start | bytes 28
  18.5 57.7 %copy-start.1 = (bf16[32,64,768]{2,1,0:T(8,128)(2,1)S(1)}, bf16[32,64,768]{2,1,0:T(8,128)(2,1)}, u32[]{:S(2)}) copy-start(bf16[32,64,768]{2,1,0:T(8,128)(2,1)} %param.9) | copy-start | bytes 9437188
  60.9 234.6 %reduce-scatter.4.cloned.1.call-start = ((), (), s32[]{:S(2)}) async-start(), calls=%async_computation.4 | async-start | bytes 245760
  133.9 3.3 copy-start.2
  133.9 3.3 copy-start.3
  133.9 4.2 copy-start.4
  302.7 39.1 %all-to-all-start.1 = ((bf16[192,64,32]{0,2,1:T(8,128)(2,1)}), bf16[192,64,32]{0,2,1:T(8,128)(2,1)}, u32[]{:S(2)}, u32[]{:S(2)}) async-start(bf16[192,64,32]{0,2,1:T(8,128)(2,1)} %bitcast.344), calls=%async_computation.1 | async-start | bytes 2097152 | tf_op jit(solution)/shard_map/all_to_all | solution.py:143
  313.4 197.2 %all-reduce.3.cloned.1.call-start = ((), (), s32[]{:S(2)}) async-start(), calls=%async_computation.5 | async-start | bytes 3538944 | tf_op jit(solution)/shard_map/psum | solution.py:133
  313.5 3.8 copy-start.5
Sparse Core Ops, SparseCore 0:
  61.1 38.7 all-gather.1
  273.1 22.4 reduce-scatter.3
  319.1 191.4 all-reduce.2
